TPU v7x, 512 devices: a whole 4x8x8 slice. The times are simulated.
512 devices in a mesh: ex: 64 (over y, z_hi, core), feat: 8 (over x, z_lo).
Axes of the slice: x: 4, y: 8, z: 8 (z_hi: 4, z_lo: 2; z = z_hi * 2 + z_lo), core: 2. Of those that a mesh axis runs over, the one named last changes fastest.
Arguments:
- proj_inputs: bfloat16 [2, 2048, 24, 2048], P(None, 'ex', None, 'feat'), may hold values from -6 to 6
- out_cotangent: bfloat16 [2, 2048, 24, 4096], P(None, 'ex', None, 'feat'), may hold values from -200 to 200
- seq_lengths: int32 [2048], P('ex'), may hold values from 6 to 24, as said below
- frozen_adapter: bfloat16 [2, 128, 2048], P(None, None, 'feat'), may hold values from -0.125 to 0.125
- left_factor: bfloat16 [2, 512, 4096], P(None, None, 'feat'), may hold values from -0.09375 to 0.09375
- right_factor: bfloat16 [2, 128, 16], replicated, may hold values from -0.5 to 0.5
- valid_grads: bfloat16 [256, 8192], P('ex', 'feat'), may hold values from -200 to 200
Outputs:
- scores: float32 [2048, 256], P('ex')
Inputs may be any that keep to these rules, and one draw needn't show every extreme that they name: Tokens at positions below seq_lengths are live; in every aligned block of 32 examples one example has all 24 tokens live and one has the fewest allowed.
All inputs are finite; a program needn't handle non-finite values.
Results may differ from a plain program's by a relative error of at most 0.0037.
Values may be sent and summed in bfloat16 or wider, within the bound.
No kernel may reach another device: no remote copies, remote signals or barrier semaphores. Data moves between devices by JAX's collectives and lax.ppermute only.
A program may use at most 64 MiB of HBM per device.

v0:
```python
import math
import jax
import jax.numpy as jnp
from jax import lax
from jax.sharding import PartitionSpec as P


def body(
    proj_inputs, out_cotangent, seq_lengths, frozen_adapter, left_factor, right_factor, valid_grads
):
    highest = lax.Precision.HIGHEST
    layer_count, example_count, token_count, _ = proj_inputs.shape
    feat_count = lax.axis_size("feat")
    proj_count = right_factor.shape[2]
    owned_rows = left_factor.shape[1] // feat_count
    position = jnp.arange(token_count, dtype=jnp.int32)
    live_tokens = (position[None, :] < seq_lengths[:, None]).astype(jnp.float32)
    adapted = jnp.einsum(
        "lesh,lrh->lesr", proj_inputs, frozen_adapter, preferred_element_type=jnp.float32
    )
    right_wide = right_factor.astype(jnp.float32)
    adapted = lax.psum(adapted, "feat")
    right_rows = jnp.einsum("lesr,lrb->lesb", adapted, right_wide, precision=highest)
    right_rows = (right_rows * live_tokens[None, :, :, None]).astype(jnp.bfloat16)
    flat_cotan = out_cotangent.reshape(
        layer_count, example_count * token_count, out_cotangent.shape[3]
    )
    term = jnp.einsum("lkd,ltd->klt", left_factor, flat_cotan, preferred_element_type=jnp.float32)
    left_rows = lax.psum_scatter(
        term.reshape(lax.axis_size("feat") * owned_rows, layer_count * example_count * token_count),
        "feat",
        scatter_dimension=0,
        tiled=True,
    )
    own_rows = left_rows.shape[0]
    left_rows = left_rows.reshape(own_rows, layer_count, example_count, token_count)
    projected = jnp.einsum(
        "kles,lesb->ekb", left_rows, right_rows.astype(jnp.float32), precision=highest
    )
    projected = projected.reshape(example_count, own_rows * proj_count)
    train_squares = jnp.sum(projected * projected, axis=1)
    rounded = projected.astype(jnp.bfloat16)
    scaling = math.sqrt(valid_grads.shape[1] * feat_count)
    valid_wide = valid_grads.astype(jnp.float32)
    valid_squares = jnp.sum(valid_wide * valid_wide, axis=1)
    products = jnp.einsum(
        "ek,vk->ev",
        lax.all_gather(rounded, "ex", axis=0, tiled=True),
        valid_grads,
        preferred_element_type=jnp.float32,
    )
    products, valid_squares, train_squares = lax.psum(
        (products, valid_squares, train_squares), "feat"
    )
    products = products / jnp.sqrt(valid_squares + 1e-06)[None, :]
    products = lax.all_to_all(products, "ex", split_axis=0, concat_axis=1, tiled=True)
    return scaling * products / jnp.sqrt(train_squares + 1e-06)[:, None]


def solution(mesh):
    return jax.shard_map(
        body,
        mesh=mesh,
        in_specs=(
            P(None, "ex", None, "feat"),
            P(None, "ex", None, "feat"),
            P("ex"),
            P(None, None, "feat"),
            P(None, None, "feat"),
            P(),
            P("ex", "feat"),
        ),
        out_specs=P("ex", None),
        check_vma=False,
    )
```

profile of v0, /device:TPU:1, one launch (start us, length us, event | category | flops | bytes accessed | tf_op | source)
XLA Modules:
  0.0 342.0 jit_solution(11740228024214441054)
XLA Ops:
  6.5 0.0 copy-start
  6.5 0.0 copy-start.1
  6.5 0.0 all-reduce.3.cloned.1.call-start
  6.5 2.5 fusion.3
  9.1 0.0 all-reduce.3.cloned.1.call-update
  9.1 0.0 reduce-scatter.4.cloned.1.call-start
  9.1 0.0 copy-done
  9.2 0.0 copy-done.1
  9.2 2.7 fusion.7
  11.9 3.5 %copy.20 = f32[512,1536]{1,0:T(8,128)} copy(f32[512,1536]{0,1:T(8,128)} %bitcast.34) | data formatting | bytes 6291456
  15.4 0.0 copy-start.4
  15.4 0.0 copy-start.3
  15.4 0.0 copy-start.2
  15.4 0.0 reduce-scatter.4.cloned.1.call-update
  15.5 0.0 all-gather.2.cloned.1.call-start
  15.5 0.6 copy-done.4
  16.1 0.1 fusion.5
  16.2 83.7 %all-reduce.3.cloned.1.call-done = f32[2,32,24,128]{3,2,1,0:T(8,128)} async-done(((f32[2,32,24,128]{3,2,1,0:T(8,128)}), f32[2,32,24,128]{3,2,1,0:T(8,128)}) %all-reduce.3.cloned.1.call-update) | async-done | bytes 786448 | tf_op jit(solution)/shard_map/psum | solution.py:22
  99.8 0.0 copy-done.3
  99.8 3.2 fusion
  103.0 80.2 %reduce-scatter.4.cloned.1.call-done = f32[64,1536]{1,0:T(8,128)} async-done(((f32[512,1536]{1,0:T(8,128)}), f32[64,1536]{1,0:T(8,128)}) %reduce-scatter.4.cloned.1.call-update) | async-done | bytes 393232
  183.2 1.3 copy.21
  184.5 0.8 multiply_reduce_fusion
  185.3 0.3 copy.15
  185.6 0.8 copy.16
  186.3 0.0 all-gather.2.cloned.1.call-update
  186.3 0.0 copy-done.2
  186.4 0.1 multiply_reduce_fusion.1
  186.5 88.7 %all-gather.2.cloned.1.call-done = bf16[2048,1024]{1,0:T(8,128)(2,1)} async-done(((bf16[32,1024]{1,0:T(8,128)(2,1)}), bf16[2048,1024]{1,0:T(8,128)(2,1)}) %all-gather.2.cloned.1.call-update) | async-done | bytes 4194320 | tf_op jit(solution)/shard_map/all_gather | solution.py:48
  275.2 3.4 fusion.8
  278.6 28.1 %all-reduce = (f32[2048,4]{0,1:T(4,128)S(1)}, f32[4]{0:T(128)S(1)}, f32[32]{0:T(128)S(1)}) all-reduce(f32[2048,4]{0,1:T(4,128)S(1)} %fusion.8, f32[4]{0:T(128)S(1)} %multiply_reduce_fusion.1, f32[32]{0:T(128)S(1)} %get-tuple-element.8), channel_id=1, replica_groups=mesh['ex'=64,'feat'=8] {'feat'}, use_global_device_ids=true, to_apply=%region_2.0 | all-reduce | flops 8228 | bytes 65824 | tf_op jit(solution)/shard_map/psum | solution.py:52
  306.7 0.1 broadcast_divide_fusion.1
  306.7 0.1 all_to_all.10
  306.8 0.1 copy.29
  306.9 0.8 reshape.48
  307.7 13.9 %all-to-all-start = ((f32[64,1,128]{2,1,0:T(1,128)}), f32[64,1,128]{2,1,0:T(1,128)S(1)}, u32[]{:S(2)}, u32[]{:S(2)}) async-start(f32[64,1,128]{2,1,0:T(1,128)} %reshape.48), calls=%async_computation | async-start | bytes 65536 | tf_op jit(solution)/shard_map/all_to_all | solution.py:56
  321.7 11.7 %all-to-all-done = f32[64,1,128]{2,1,0:T(1,128)S(1)} async-done(((f32[64,1,128]{2,1,0:T(1,128)}), f32[64,1,128]{2,1,0:T(1,128)S(1)}, u32[]{:S(2)}, u32[]{:S(2)}) %all-to-all-start) | async-done | bytes 32800 | tf_op jit(solution)/shard_map/all_to_all | solution.py:56
  333.4 0.5 broadcast.25
  333.9 0.7 reduce.1
  334.6 0.1 reshape.49
  334.8 0.7 copy.18
  (4 shorter events, 0.1 us)
Async XLA Ops:
  6.5 2.6 copy-start
  6.5 2.6 copy-start.1
  6.5 93.3 %all-reduce.3.cloned.1.call-start = ((), (), s32[]{:S(2)}) async-start(), calls=%async_computation.2 | async-start | bytes 1572864 | tf_op jit(solution)/shard_map/psum | solution.py:22
  9.1 174.1 %reduce-scatter.4.cloned.1.call-start = ((), (), s32[]{:S(2)}) async-start(), calls=%async_computation.4 | async-start | bytes 3538944
  15.4 0.7 copy-start.4
  15.4 84.4 %copy-start.3 = (bf16[2,128,16]{1,2,0:T(8,128)(2,1)S(1)}, bf16[2,128,16]{1,2,0:T(8,128)(2,1)}, u32[]{:S(2)}) copy-start(bf16[2,128,16]{1,2,0:T(8,128)(2,1)} %param.12) | copy-start | bytes 24580
  15.4 170.9 %copy-start.2 = (bf16[4,1024]{1,0:T(4,128)(2,1)S(1)}, bf16[4,1024]{1,0:T(4,128)(2,1)}, u32[]{:S(2)}) copy-start(bf16[4,1024]{1,0:T(4,128)(2,1)} %param.13) | copy-start | bytes 24580
  15.5 259.8 %all-gather.2.cloned.1.call-start = ((), (), s32[]{:S(2)}) async-start(), calls=%async_computation.3 | async-start | bytes 4259840 | tf_op jit(solution)/shard_map/all_gather | solution.py:48
  307.7 25.7 %all-to-all-start = ((f32[64,1,128]{2,1,0:T(1,128)}), f32[64,1,128]{2,1,0:T(1,128)S(1)}, u32[]{:S(2)}, u32[]{:S(2)}) async-start(f32[64,1,128]{2,1,0:T(1,128)} %reshape.48), calls=%async_computation | async-start | bytes 65536 | tf_op jit(solution)/shard_map/all_to_all | solution.py:56
Sparse Core Ops, SparseCore 0:
  10.3 89.4 all-reduce.2
  102.7 80.5 reduce-scatter.3
  186.5 88.6 all-gather.1
where the time goes:
time: 342 us
  waiting for transfers between devices  264 us (77%)
  blocking collectives  28.1 us (8%)
  starting transfers between devices  14 us (4%)
  between operations  13.2 us (4%)
  matrix products  12.6 us (4%)
  local copies, waits for them, and re-layouts  8.7 us (3%)
    all_gather x1, waiting for transfers between devices, body(): lax.all_gather(rounded, 'ex', axis=0, tiled=True)  88.7 us
    psum x1, waiting for transfers between devices, body(): adapted = lax.psum(adapted, 'feat')  83.7 us
    unnamed x4, waiting for transfers between devices  80.3 us
    psum x1, blocking collectives, body(): lax.psum((products, valid_squares, train_squares), 'feat')  28.1 us
    all_to_all x1, starting transfers between devices, body(): lax.all_to_all(products, 'ex', split_axis=0, concat_axis=1, tiled=True)  13.9 us
    all_to_all x1, waiting for transfers between devices, body(): lax.all_to_all(products, 'ex', split_axis=0, concat_axis=1, tiled=True)  11.7 us
  transfers between devices with their start and end apart: 4, of which 4 were waited for; matrix products, arithmetic and copies ran while one was open for 3% of the time, Pallas kernels for 0%

commit v1 on v0

--- a/solution.py
+++ b/solution.py
@@ -19,7 +19,8 @@
         "lesh,lrh->lesr", proj_inputs, frozen_adapter, preferred_element_type=jnp.float32
     )
     right_wide = right_factor.astype(jnp.float32)
-    adapted = lax.psum(adapted, "feat")
+    blocks = lax.all_gather(adapted, "feat")
+    adapted = jnp.sum(blocks, axis=0)
     right_rows = jnp.einsum("lesr,lrb->lesb", adapted, right_wide, precision=highest)
     right_rows = (right_rows * live_tokens[None, :, :, None]).astype(jnp.bfloat16)
     flat_cotan = out_cotangent.reshape(

time: 342 us -> 399 us (1.17)
  waiting for transfers between devices: 264 us -> 317 us
    all_gather x0 -> x1, waiting for transfers between devices: none -> 135 us  [body(): blocks = lax.all_gather(adapted, 'feat')]
    psum x1 -> x0, waiting for transfers between devices: 83.7 us -> none  [body(): adapted = lax.psum(adapted, 'feat')]
    unnamed x14 -> x16, local copies, waits for them, and re-layouts: 6.26 us -> 8.19 us
  transfers between devices with their start and end apart: 4 -> 4, of which waited for: 4 -> 4; matrix products, arithmetic and copies ran while one was open for 3% -> 1% of each run, Pallas kernels for 0% -> 0%
where the time goes in v1:
time: 399 us; the launch traced here: 398 us
  waiting for transfers between devices  317 us (79%)
  blocking collectives  28.1 us (7%)
  starting transfers between devices  14 us (4%)
  between operations  13.2 us (3%)
  matrix products  11.3 us (3%)
  local copies, waits for them, and re-layouts  10.6 us (3%)
  other arithmetic  4.24 us (1%)
    all_gather x1, waiting for transfers between devices, body(): blocks = lax.all_gather(adapted, 'feat')  135 us
    all_gather x1, waiting for transfers between devices, body(): lax.all_gather(rounded, 'ex', axis=0, tiled=True)  89.8 us
    unnamed x4, waiting for transfers between devices  80.2 us
    psum x1, blocking collectives, body(): lax.psum((products, valid_squares, train_squares), 'feat')  28.1 us
    all_to_all x1, starting transfers between devices, body(): lax.all_to_all(products, 'ex', split_axis=0, concat_axis=1, tiled=True)  13.9 us
    all_to_all x1, waiting for transfers between devices, body(): lax.all_to_all(products, 'ex', split_axis=0, concat_axis=1, tiled=True)  11.7 us
    unnamed x16, local copies, waits for them, and re-layouts  8.19 us
  transfers between devices with their start and end apart: 4, of which 4 were waited for; matrix products, arithmetic and copies ran while one was open for 1% of the time, Pallas kernels for 0%

profile of v1, /device:TPU:1, one launch (start us, length us, event | category | flops | bytes accessed | tf_op | source)
XLA Modules:
  0.0 398.2 jit_solution(14142326388233238354)
XLA Ops:
  6.5 0.0 copy-start
  6.5 0.0 reduce-scatter.4.cloned.1.call-start
  6.5 1.4 copy-done
  7.9 3.9 fusion.7
  11.8 3.6 copy.25
  15.4 0.0 copy-start.1
  15.4 0.0 copy-start.2
  15.4 0.0 copy-start.5
  15.4 0.0 reduce-scatter.4.cloned.1.call-update
  15.4 0.0 all-gather.6.cloned.1.call-start
  15.5 1.1 copy-done.1
  16.6 0.0 copy-done.2
  16.6 1.3 fusion.3
  17.8 0.0 all-gather.6.cloned.1.call-update
  17.8 0.0 all-gather.4.cloned.1.call-start
  17.9 0.0 copy-done.5
  17.9 0.1 fusion.5
  18.0 80.2 %reduce-scatter.4.cloned.1.call-done = f32[64,1536]{1,0:T(8,128)} async-done(((f32[512,1536]{1,0:T(8,128)}), f32[64,1536]{1,0:T(8,128)}) %reduce-scatter.4.cloned.1.call-update) | async-done | bytes 393232
  98.1 1.3 copy.26
  99.4 135.0 %all-gather.6.cloned.1.call-done = f32[16,32,24,128]{3,2,1,0:T(8,128)} async-done(((f32[2,32,24,128]{3,2,1,0:T(8,128)}), f32[16,32,24,128]{3,2,1,0:T(8,128)}) %all-gather.6.cloned.1.call-update) | async-done | bytes 6291472 | tf_op jit(solution)/shard_map/all_gather | solution.py:22
  234.4 0.0 copy-start.4
  234.4 0.0 copy-start.3
  234.4 3.2 reduce_sum.27
  237.6 0.0 copy-done.4
  237.6 2.1 fusion
  239.7 0.8 multiply_reduce_fusion
  240.5 0.3 copy.20
  240.8 0.8 copy.21
  241.5 0.0 all-gather.4.cloned.1.call-update
  241.5 0.0 copy-done.3
  241.5 0.1 multiply_reduce_fusion.1
  241.7 89.8 %all-gather.4.cloned.1.call-done = bf16[2048,1024]{1,0:T(8,128)(2,1)} async-done(((bf16[32,1024]{1,0:T(8,128)(2,1)}), bf16[2048,1024]{1,0:T(8,128)(2,1)}) %all-gather.4.cloned.1.call-update) | async-done | bytes 4194320 | tf_op jit(solution)/shard_map/all_gather | solution.py:49
  331.4 3.4 fusion.8
  334.8 28.1 %all-reduce = (f32[2048,4]{0,1:T(4,128)S(1)}, f32[4]{0:T(128)S(1)}, f32[32]{0:T(128)S(1)}) all-reduce(f32[2048,4]{0,1:T(4,128)S(1)} %fusion.8, f32[4]{0:T(128)S(1)} %multiply_reduce_fusion.1, f32[32]{0:T(128)S(1)} %get-tuple-element.8), channel_id=1, replica_groups=mesh['ex'=64,'feat'=8] {'feat'}, use_global_device_ids=true, to_apply=%region_2.0 | all-reduce | flops 8228 | bytes 65824 | tf_op jit(solution)/shard_map/psum | solution.py:53
  362.9 0.1 broadcast_divide_fusion.1
  363.0 0.1 all_to_all.10
  363.1 0.1 copy.34
  363.2 0.8 reshape.49
  363.9 13.9 %all-to-all-start = ((f32[64,1,128]{2,1,0:T(1,128)}), f32[64,1,128]{2,1,0:T(1,128)S(1)}, u32[]{:S(2)}, u32[]{:S(2)}) async-start(f32[64,1,128]{2,1,0:T(1,128)} %reshape.49), calls=%async_computation | async-start | bytes 65536 | tf_op jit(solution)/shard_map/all_to_all | solution.py:57
  377.9 11.7 %all-to-all-done = f32[64,1,128]{2,1,0:T(1,128)S(1)} async-done(((f32[64,1,128]{2,1,0:T(1,128)}), f32[64,1,128]{2,1,0:T(1,128)S(1)}, u32[]{:S(2)}, u32[]{:S(2)}) %all-to-all-start) | async-done | bytes 32800 | tf_op jit(solution)/shard_map/all_to_all | solution.py:57
  389.6 0.5 broadcast.25
  390.1 0.7 reduce.1
  390.8 0.1 reshape.50
  391.0 0.7 copy.23
  (4 shorter events, 0.1 us)
Async XLA Ops:
  6.5 1.4 copy-start
  6.5 91.6 %reduce-scatter.4.cloned.1.call-start = ((), (), s32[]{:S(2)}) async-start(), calls=%async_computation.4 | async-start | bytes 3538944
  15.4 1.1 copy-start.1
  15.4 1.1 copy-start.2
  15.4 2.5 copy-start.5
  15.4 219.0 %all-gather.6.cloned.1.call-start = ((), (), s32[]{:S(2)}) async-start(), calls=%async_computation.3 | async-start | bytes 7077888 | tf_op jit(solution)/shard_map/all_gather | solution.py:22
  17.8 313.6 %all-gather.4.cloned.1.call-start = ((), (), s32[]{:S(2)}) async-start(), calls=%async_computation.2 | async-start | bytes 4259840 | tf_op jit(solution)/shard_map/all_gather | solution.py:49
  234.4 3.2 copy-start.4
  234.4 7.1 %copy-start.3 = (bf16[4,1024]{1,0:T(4,128)(2,1)S(1)}, bf16[4,1024]{1,0:T(4,128)(2,1)}, u32[]{:S(2)}) copy-start(bf16[4,1024]{1,0:T(4,128)(2,1)} %param.13) | copy-start | bytes 24580
  363.9 25.7 %all-to-all-start = ((f32[64,1,128]{2,1,0:T(1,128)}), f32[64,1,128]{2,1,0:T(1,128)S(1)}, u32[]{:S(2)}, u32[]{:S(2)}) async-start(f32[64,1,128]{2,1,0:T(1,128)} %reshape.49), calls=%async_computation | async-start | bytes 65536 | tf_op jit(solution)/shard_map/all_to_all | solution.py:57
Sparse Core Ops, SparseCore 0:
  15.6 82.5 reduce-scatter.3
  100.2 134.1 all-gather.5
  241.7 89.7 all-gather.3

commit v2 on v0

--- a/solution.py
+++ b/solution.py
@@ -3,6 +3,13 @@
 import jax.numpy as jnp
 from jax import lax
 from jax.sharding import PartitionSpec as P
+
+
+def exchange_gather(block, axis, d):
+    size = lax.axis_size(axis)
+    tiles = jnp.stack([block for _ in range(size)])
+    tiles = lax.all_to_all(tiles, axis, split_axis=0, concat_axis=0)
+    return jnp.concatenate(tiles, axis=d)
 
 
 def body(
@@ -45,7 +52,7 @@
     valid_squares = jnp.sum(valid_wide * valid_wide, axis=1)
     products = jnp.einsum(
         "ek,vk->ev",
-        lax.all_gather(rounded, "ex", axis=0, tiled=True),
+        exchange_gather(rounded, "ex", 0),
         valid_grads,
         preferred_element_type=jnp.float32,
     )

time: 342 us -> 393 us (1.15)
  starting transfers between devices: 14 us -> 47.3 us
  waiting for transfers between devices: 264 us -> 279 us
    all_to_all x0 -> x1, waiting for transfers between devices: none -> 104 us  [exchange_gather(): tiles = lax.all_to_all(tiles, axis, split_axis=0, concat_axis=0)]
    all_gather x1 -> x0, waiting for transfers between devices: 88.7 us -> none  [body(): lax.all_gather(rounded, 'ex', axis=0, tiled=True)]
    all_to_all x1, starting transfers between devices: 13.9 us -> 34 us  [body(): lax.all_to_all(products, 'ex', split_axis=0, concat_axis=1, tiled=True)]
    all_to_all x0 -> x1, starting transfers between devices: none -> 13.3 us  [exchange_gather(): tiles = lax.all_to_all(tiles, axis, split_axis=0, concat_axis=0)]
    unnamed x4 -> x3, waiting for transfers between devices: 80.3 us -> 80.3 us
  transfers between devices with their start and end apart: 4 -> 4, of which waited for: 4 -> 4; matrix products, arithmetic and copies ran while one was open for 3% -> 2% of each run, Pallas kernels for 0% -> 0%
where the time goes in v2:
time: 393 us
  waiting for transfers between devices  279 us (71%)
  starting transfers between devices  47.3 us (12%)
  blocking collectives  28.4 us (7%)
  between operations  13.5 us (3%)
  matrix products  12.6 us (3%)
  local copies, waits for them, and re-layouts  10.6 us (3%)
    all_to_all x1, waiting for transfers between devices, exchange_gather(): tiles = lax.all_to_all(tiles, axis, split_axis=0, concat_axis=0)  104 us
    psum x1, waiting for transfers between devices, body(): adapted = lax.psum(adapted, 'feat')  83.7 us
    unnamed x3, waiting for transfers between devices  80.3 us
    all_to_all x1, starting transfers between devices, body(): lax.all_to_all(products, 'ex', split_axis=0, concat_axis=1, tiled=True)  34 us
    psum x1, blocking collectives, body(): lax.psum((products, valid_squares, train_squares), 'feat')  28.4 us
    all_to_all x1, starting transfers between devices, exchange_gather(): tiles = lax.all_to_all(tiles, axis, split_axis=0, concat_axis=0)  13.3 us
    all_to_all x1, waiting for transfers between devices, body(): lax.all_to_all(products, 'ex', split_axis=0, concat_axis=1, tiled=True)  11.7 us
  transfers between devices with their start and end apart: 4, of which 4 were waited for; matrix products, arithmetic and copies ran while one was open for 2% of the time, Pallas kernels for 0%

profile of v2, /device:TPU:1, one launch (start us, length us, event | category | flops | bytes accessed | tf_op | source)
XLA Modules:
  0.0 392.9 jit_solution(16814512929769145363)
XLA Ops:
  6.5 0.0 copy-start
  6.5 0.0 copy-start.1
  6.5 0.0 all-reduce.3.cloned.1.call-start
  6.5 2.5 fusion.3
  9.1 0.0 all-reduce.3.cloned.1.call-update
  9.1 0.0 reduce-scatter.4.cloned.1.call-start
  9.1 0.0 copy-done
  9.2 0.0 copy-done.1
  9.2 2.7 fusion.7
  11.9 3.5 copy.21
  15.4 0.0 copy-start.4
  15.4 0.0 copy-start.3
  15.4 0.0 reduce-scatter.4.cloned.1.call-update
  15.5 0.6 copy-done.4
  16.1 0.1 fusion.5
  16.2 83.7 %all-reduce.3.cloned.1.call-done = f32[2,32,24,128]{3,2,1,0:T(8,128)} async-done(((f32[2,32,24,128]{3,2,1,0:T(8,128)}), f32[2,32,24,128]{3,2,1,0:T(8,128)}) %all-reduce.3.cloned.1.call-update) | async-done | bytes 786448 | tf_op jit(solution)/shard_map/psum | solution.py:29
  99.8 0.0 copy-done.3
  99.8 3.2 fusion
  103.0 80.2 %reduce-scatter.4.cloned.1.call-done = f32[64,1536]{1,0:T(8,128)} async-done(((f32[512,1536]{1,0:T(8,128)}), f32[64,1536]{1,0:T(8,128)}) %reduce-scatter.4.cloned.1.call-update) | async-done | bytes 393232
  183.2 1.3 copy.22
  184.5 0.8 multiply_reduce_fusion
  185.3 0.3 copy.16
  185.6 0.1 copy.17
  185.7 2.5 stack.2
  188.2 0.0 copy-start.2
  188.2 13.3 %all-to-all-start = ((bf16[64,32,1024]{2,1,0:T(8,128)(2,1)}), bf16[64,32,1024]{2,1,0:T(8,128)(2,1)}, u32[]{:S(2)}, u32[]{:S(2)}) async-start(bf16[64,32,1024]{2,1,0:T(8,128)(2,1)} %stack.2), calls=%async_computation | async-start | bytes 8388608 | tf_op jit(solution)/shard_map/all_to_all | solution.py:11
  201.5 0.0 copy-done.2
  201.5 0.1 multiply_reduce_fusion.1
  201.7 103.8 %all-to-all-done = bf16[64,32,1024]{2,1,0:T(8,128)(2,1)} async-done(((bf16[64,32,1024]{2,1,0:T(8,128)(2,1)}), bf16[64,32,1024]{2,1,0:T(8,128)(2,1)}, u32[]{:S(2)}, u32[]{:S(2)}) %all-to-all-start) | async-done | bytes 4194336 | tf_op jit(solution)/shard_map/all_to_all | solution.py:11
  305.5 3.4 fusion.8
  308.8 28.4 %all-reduce = (f32[2048,4]{0,1:T(4,128)S(1)}, f32[4]{0:T(128)S(1)}, f32[32]{0:T(128)S(1)}) all-reduce(f32[2048,4]{0,1:T(4,128)S(1)} %fusion.8, f32[4]{0:T(128)S(1)} %multiply_reduce_fusion.1, f32[32]{0:T(128)S(1)} %get-tuple-element.8), channel_id=1, replica_groups=mesh['ex'=64,'feat'=8] {'feat'}, use_global_device_ids=true, to_apply=%region_2.0 | all-reduce | flops 8228 | bytes 65824 | tf_op jit(solution)/shard_map/psum | solution.py:59
  337.2 0.1 broadcast_divide_fusion.1
  337.3 0.1 all_to_all.14
  337.4 0.1 copy.30
  337.5 0.8 reshape.55
  338.2 34.0 %all-to-all-start.1 = ((f32[64,1,128]{2,1,0:T(1,128)}), f32[64,1,128]{2,1,0:T(1,128)S(1)}, u32[]{:S(2)}, u32[]{:S(2)}) async-start(f32[64,1,128]{2,1,0:T(1,128)} %reshape.55), calls=%async_computation.1 | async-start | bytes 65536 | tf_op jit(solution)/shard_map/all_to_all | solution.py:63
  372.2 11.7 %all-to-all-done.1 = f32[64,1,128]{2,1,0:T(1,128)S(1)} async-done(((f32[64,1,128]{2,1,0:T(1,128)}), f32[64,1,128]{2,1,0:T(1,128)S(1)}, u32[]{:S(2)}, u32[]{:S(2)}) %all-to-all-start.1) | async-done | bytes 32800 | tf_op jit(solution)/shard_map/all_to_all | solution.py:63
  383.9 0.5 broadcast.26
  384.4 0.7 reduce.1
  385.2 0.1 reshape.56
  385.4 0.7 copy.19
  (4 shorter events, 0.1 us)
Async XLA Ops:
  6.5 2.6 copy-start
  6.5 2.6 copy-start.1
  6.5 93.3 %all-reduce.3.cloned.1.call-start = ((), (), s32[]{:S(2)}) async-start(), calls=%async_computation.3 | async-start | bytes 1572864 | tf_op jit(solution)/shard_map/psum | solution.py:29
  9.1 174.1 %reduce-scatter.4.cloned.1.call-start = ((), (), s32[]{:S(2)}) async-start(), calls=%async_computation.4 | async-start | bytes 3538944
  15.4 0.7 copy-start.4
  15.4 84.4 %copy-start.3 = (bf16[2,128,16]{1,2,0:T(8,128)(2,1)S(1)}, bf16[2,128,16]{1,2,0:T(8,128)(2,1)}, u32[]{:S(2)}) copy-start(bf16[2,128,16]{1,2,0:T(8,128)(2,1)} %param.12) | copy-start | bytes 24580
  188.2 13.3 %copy-start.2 = (bf16[4,1024]{1,0:T(4,128)(2,1)S(1)}, bf16[4,1024]{1,0:T(4,128)(2,1)}, u32[]{:S(2)}) copy-start(bf16[4,1024]{1,0:T(4,128)(2,1)} %param.13) | copy-start | bytes 24580
  188.2 117.3 %all-to-all-start = ((bf16[64,32,1024]{2,1,0:T(8,128)(2,1)}), bf16[64,32,1024]{2,1,0:T(8,128)(2,1)}, u32[]{:S(2)}, u32[]{:S(2)}) async-start(bf16[64,32,1024]{2,1,0:T(8,128)(2,1)} %stack.2), calls=%async_computation | async-start | bytes 8388608 | tf_op jit(solution)/shard_map/all_to_all | solution.py:11
  338.2 45.7 %all-to-all-start.1 = ((f32[64,1,128]{2,1,0:T(1,128)}), f32[64,1,128]{2,1,0:T(1,128)S(1)}, u32[]{:S(2)}, u32[]{:S(2)}) async-start(f32[64,1,128]{2,1,0:T(1,128)} %reshape.55), calls=%async_computation.1 | async-start | bytes 65536 | tf_op jit(solution)/shard_map/all_to_all | solution.py:63
Sparse Core Ops, SparseCore 0:
  10.3 89.4 all-reduce.2
  102.7 80.5 reduce-scatter.3
